TPU v7x, 512 devices: a whole 4x8x8 slice. The times are simulated.
512 devices in a mesh: replica: 64 (over x, y, core), tensor: 8 (over z).
Axes of the slice: x: 4, y: 8, z: 8, core: 2. Of those that a mesh axis runs over, the one named last changes fastest.
Arguments:
- features: bfloat16 [4096, 4, 7680], P('replica', None, 'tensor'), may hold values from -6 to 6
- kv_weight: bfloat16 [7680, 8, 256], P('tensor'), may hold values from -0.0625 to 0.0625
- image_owner: int32 [4096], replicated, may hold values from 0 to 63, as said below
- image_request: int32 [4096], replicated, may hold values from 0 to 7, as said below
- cross_query: bfloat16 [512, 64, 128], P('replica', 'tensor'), may hold values from -6 to 6
- self_query: bfloat16 [512, 64, 128], P('replica', 'tensor'), may hold values from -2.5 to 2.5
- self_cache: bfloat16 [512, 128, 8, 256], P('replica', None, 'tensor'), may hold values from -2.5 to 2.5
- fresh_key_value: bfloat16 [512, 8, 256], P('replica', 'tensor'), may hold values from -2.5 to 2.5
- cache_len: int32 [512], P('replica'), may hold values from 1 to 128, 32768 in all
Outputs:
- cross_out: bfloat16 [512, 64, 128], P('replica', 'tensor')
- self_out: bfloat16 [512, 64, 128], P('replica', 'tensor')
Inputs may be any that keep to these rules, and one draw needn't show every extreme that they name: `image_owner`: within each aligned block of 64 consecutive images (the images of one replica group), no decode replica owns more than 2 images, and one decode replica owns exactly 2 images in every block. `image_request`: some requests have no image.
All inputs are finite; a program needn't handle non-finite values. No bound on the sum of `cache_len` on one device may be relied on, other than what follows from the above.
Results may differ from a plain program's by a relative error of at most 0.02.
Values may be sent and summed in bfloat16 or wider, within the bound.
No kernel may reach another device: no remote copies, remote signals or barrier semaphores. Data moves between devices by JAX's collectives and lax.ppermute only.
A program may use at most 64 MiB of HBM per device.

v0:
```python
import math

import jax
import jax.numpy as jnp
from jax import lax
from jax.experimental import pallas as pl
from jax.experimental.pallas import tpu as pltpu
from jax.sharding import PartitionSpec as P


STEP = 256
EARLY = 2


def head_order(count, outward):
    ten = lax.axis_index("tensor")
    n_ten = lax.axis_size("tensor")
    if outward:
        odd = lax.rem(ten + lax.axis_index("replica"), 2)
        ten = lax.rem(ten + jnp.where(odd == 0, 1, n_ten - 1), n_ten)
    side = lax.rem(ten, 2)
    return [lax.rem(ten // 2 + apart, count) * 2 + side for apart in (2, 1, count - 1, 0)]


def project_body(features_ref, weight_ref, *refs):
    outs, (flat, wide, raw, feat, early, sem) = refs[:4], refs[4:]
    block = weight_ref.shape[0]
    places = [(out, i) for out in outs for i in range(out.shape[0])]
    parts = [pl.ds(lo, min(STEP, block - lo)) for lo in range(0, block, STEP)]
    first = pltpu.make_async_copy(features_ref, feat, sem.at[len(parts)])
    loads = [
        pltpu.make_async_copy(weight_ref.at[part], raw.at[part], sem.at[k])
        for k, part in enumerate(parts)
    ]
    loads[0].start()
    first.start()
    for load in loads[1:]:
        load.start()
    count = len(places) // 2
    heads = head_order(count, True) + head_order(count, False)
    cut = EARLY * STEP
    for k, part in enumerate(parts):
        loads[k].wait()
        wide[:, part, :] = jnp.swapaxes(raw[part], 0, 1)
        if k == 0:
            first.wait()
            flat[...] = feat[...].reshape(flat.shape)
        if k == EARLY - 1:
            for i, head in enumerate(heads):
                early[i] = jnp.dot(
                    flat[:, :cut], wide[head, :cut, :], preferred_element_type=jnp.float32
                )
    for i, head in enumerate(heads):
        late = jnp.dot(flat[:, cut:], wide[head, cut:, :], preferred_element_type=jnp.float32)
        out, at = places[i]
        out[at] = (early[i] + late).astype(jnp.bfloat16)


def project(features, weight):
    images, patches, block = features.shape
    heads, width = weight.shape[1:]
    rows = images * patches
    counts = (1, heads // 2 - 1) * 2
    copies = pl.cdiv(block, STEP)
    return pl.pallas_call(
        project_body,
        in_specs=[pl.BlockSpec(memory_space=pltpu.HBM)] * 2,
        out_specs=(pl.BlockSpec(memory_space=pltpu.VMEM),) * 4,
        out_shape=tuple(jax.ShapeDtypeStruct((n, rows, width), jnp.bfloat16) for n in counts),
        scratch_shapes=[
            pltpu.VMEM((rows, block), jnp.bfloat16),
            pltpu.VMEM((heads, block, width), jnp.bfloat16),
            pltpu.VMEM((block, heads, width), jnp.bfloat16),
            pltpu.VMEM((images, patches, block), jnp.bfloat16),
            pltpu.VMEM((heads, rows, width), jnp.float32),
            pltpu.SemaphoreType.DMA((copies + 1,)),
        ],
        compiler_params=pltpu.CompilerParams(vmem_limit_bytes=32 << 20),
    )(
        pltpu.with_memory_space_constraint(features, pltpu.HBM),
        pltpu.with_memory_space_constraint(weight, pltpu.HBM),
    )


def place_body(slot_ref, kept_ref, got_ref, a_ref, b_ref, c_ref, out_ref):
    own = kept_ref[...].astype(jnp.float32) + got_ref[...].astype(jnp.float32)
    for ref in (a_ref, b_ref, c_ref):
        own = own + ref[...].astype(jnp.float32)
    slots = lax.broadcasted_iota(jnp.int32, (out_ref.shape[0], own.shape[0]), 0)
    placing = (slots == slot_ref[...]).astype(jnp.float32).astype(jnp.bfloat16)
    out_ref[...] = jnp.dot(
        placing, own.astype(jnp.bfloat16), preferred_element_type=jnp.float32
    ).astype(jnp.bfloat16)


def place(row_slot, kept, got, arrivals, slot_rows):
    rows, width = arrivals[0].shape
    operands = (row_slot.reshape(1, rows), kept, got, *arrivals)
    whole = pl.BlockSpec(memory_space=pltpu.VMEM)
    return pl.pallas_call(
        place_body,
        in_specs=[whole] * len(operands),
        out_specs=whole,
        out_shape=jax.ShapeDtypeStruct((slot_rows, width), jnp.bfloat16),
    )(*[pltpu.with_memory_space_constraint(x, pltpu.VMEM) for x in operands])


def attend_body(tag_ref, query_ref, kv_ref, out_ref):
    count, group, head_width = query_ref.shape
    slot_rows = kv_ref.shape[0]
    scale = 1.0 / math.sqrt(head_width)
    raw = kv_ref[:, :head_width].astype(jnp.float32)
    keys = (
        raw * lax.rsqrt(jnp.mean(raw * raw, axis=-1, keepdims=True) + 1e-05)
    ).astype(jnp.bfloat16)
    query = query_ref[...].reshape(count * group, head_width)
    scores = lax.dot_general(
        query, keys, (((1,), (1,)), ((), ())), preferred_element_type=jnp.float32
    )
    request = lax.broadcasted_iota(jnp.int32, (count * group, slot_rows), 0) // group
    mask = request == tag_ref[...]
    weight = jnp.where(mask, jnp.exp(scores * scale), 0.0)
    total = jnp.sum(weight, axis=-1, keepdims=True)
    present = jnp.max(mask.astype(jnp.float32), axis=-1, keepdims=True) > 0.0
    numer = jnp.dot(
        weight.astype(jnp.bfloat16), kv_ref[:, head_width:], preferred_element_type=jnp.float32
    )
    result = jnp.where(present, numer / jnp.where(present, total, 1.0), 0.0)
    out_ref[...] = result.astype(jnp.bfloat16).reshape(out_ref.shape)


def attend(row_tag, query, kv):
    operands = (row_tag.reshape(1, kv.shape[0]), query, kv)
    return pl.pallas_call(
        attend_body,
        in_specs=[pl.BlockSpec(memory_space=pltpu.VMEM)] * 3,
        out_shape=jax.ShapeDtypeStruct(query.shape, jnp.bfloat16),
    )(*[pltpu.with_memory_space_constraint(x, pltpu.VMEM) for x in operands])


def local(
    features,
    kv_weight,
    image_owner,
    image_request,
    cross_query,
    self_query,
    self_cache,
    fresh_key_value,
    cache_len,
):
    n_rep = lax.axis_size("replica")
    n_ten = lax.axis_size("tensor")
    me_rep = lax.axis_index("replica")
    images, patches, _ = features.shape
    kvh_all, width2 = kv_weight.shape[1:]
    head_width = width2 // 2
    score_scale = 1.0 / math.sqrt(head_width)
    slot_cap = max(2, 2 * images // n_rep)
    slot_all = n_rep * slot_cap
    rows = images * patches
    req_count, sq_heads, _ = self_query.shape
    kvh_local = self_cache.shape[2]
    group = sq_heads // kvh_local

    quarter = kvh_all // 2
    neighbours = []
    for r in range(n_rep):
        for z in range(n_ten):
            step = 1 if (z + r) % 2 == 0 else -1
            neighbours.append((r * n_ten + z, r * n_ten + (z + step) % n_ten))
    both = ("replica", "tensor")
    sent_a, sent_b, kept_a, kept_b = project(features, kv_weight)
    got_a = lax.ppermute(sent_a, both, neighbours)
    got_b = lax.ppermute(sent_b, both, neighbours)

    def onward(kept, got, step):
        outward = (kept.astype(jnp.float32) + got.astype(jnp.float32)).astype(jnp.bfloat16)
        return lax.ppermute(outward, "tensor", [(z, (z + 2 * step) % n_ten) for z in range(n_ten)])

    arrivals = (
        onward(kept_a[0], got_a[0], 2),
        onward(kept_b[0], got_b[0], 1),
        onward(kept_b[1], got_b[1], quarter - 1),
    )

    owners = image_owner.reshape(n_rep, images)
    requests = image_request.reshape(n_rep, images)
    own_block = lax.dynamic_index_in_dim(owners, me_rep, 0, keepdims=False)
    positions = jnp.arange(images, dtype=jnp.int32)
    same_owner = own_block[:, None] == own_block[None, :]
    earlier = positions[:, None] > positions[None, :]
    rank = jnp.sum((same_owner & earlier).astype(jnp.int32), axis=1, dtype=jnp.int32)
    slot = own_block * slot_cap + rank
    row_slot = (slot[:, None] * patches + jnp.arange(patches, dtype=jnp.int32)[None, :]).reshape(rows)
    outgoing = place(row_slot, kept_b[2], got_b[2], arrivals, slot_all * patches)
    outgoing = outgoing.reshape(n_rep, slot_cap * patches, width2)
    arrived = lax.all_to_all(outgoing, "replica", split_axis=0, concat_axis=0, tiled=True)

    self_query_rows = self_query.reshape(req_count, kvh_local, group, head_width)
    scores = (
        jnp.einsum(
            "bkgd,bskd->bkgs",
            self_query_rows,
            self_cache[..., :head_width],
            preferred_element_type=jnp.float32,
        )
        * score_scale
    )
    live = jnp.arange(self_cache.shape[1], dtype=jnp.int32)[None, :] < cache_len[:, None]
    weight = jnp.where(live[:, None, None, :], jnp.exp(scores), jnp.float32(0.0))
    fresh_weight = jnp.exp(
        jnp.einsum(
            "ptwe,pte->ptw",
            self_query_rows,
            fresh_key_value[..., :head_width],
            preferred_element_type=jnp.float32,
        )
        * score_scale
    )
    total = jnp.sum(weight, axis=-1) + fresh_weight
    numer = jnp.einsum(
        "bkgs,bskd->bkgd",
        weight.astype(jnp.bfloat16),
        self_cache[..., head_width:],
        preferred_element_type=jnp.float32,
    )
    numer = numer + fresh_weight.astype(jnp.bfloat16).astype(jnp.float32)[
        ..., None
    ] * fresh_key_value[:, :, None, head_width:].astype(jnp.float32)
    self_out = (
        (numer / total[..., None]).astype(jnp.bfloat16).reshape(req_count, sq_heads, head_width)
    )

    owner_match = (owners == me_rep).astype(jnp.int32)
    rank_all = jnp.cumsum(owner_match, axis=1, dtype=jnp.int32) - owner_match
    slot_ids = jnp.arange(slot_cap, dtype=jnp.int32)
    chosen = owner_match[:, None, :] * (rank_all[:, None, :] == slot_ids[None, :, None]).astype(
        jnp.int32
    )
    slot_live = jnp.sum(chosen, axis=-1, dtype=jnp.int32)
    slot_req = jnp.sum(chosen * requests[:, None, :], axis=-1, dtype=jnp.int32)
    slot_tag = jnp.where(slot_live > 0, slot_req, -1)
    row_tag = jnp.broadcast_to(slot_tag[:, :, None], (n_rep, slot_cap, patches)).reshape(
        slot_all * patches
    )
    cross_out = attend(row_tag, cross_query, arrived.reshape(slot_all * patches, width2))
    return (cross_out, self_out)


def solution(mesh):
    return jax.shard_map(
        local,
        mesh=mesh,
        in_specs=(
            P("replica", None, "tensor"),
            P("tensor", None, None),
            P(),
            P(),
            P("replica", "tensor", None),
            P("replica", "tensor", None),
            P("replica", None, "tensor", None),
            P("replica", "tensor", None),
            P("replica"),
        ),
        out_specs=(P("replica", "tensor", None), P("replica", "tensor", None)),
        check_vma=False,
    )
```

profile of v0, /device:TPU:1, one launch (start us, length us, event | category | flops | bytes accessed | tf_op | source)
XLA Modules:
  0.0 67.3 jit_solution(12313537942905282457)
XLA Ops:
  0.7 3.8 %shard_map.104 = (bf16[1,256,256]{2,1,0:T(8,128)(2,1)S(1)}, bf16[3,256,256]{2,1,0:T(8,128)(2,1)S(1)}, bf16[1,256,256]{2,1,0:T(8,128)(2,1)S(1)}, bf16[3,256,256]{2,1,0:T(8,128)(2,1)S(1)}) custom-call(bf16[64,4,960]{2,1,0:T(4,128)(2,1)} %features_ref.1, bf16[960,8,256]{2,1,0:T(8,128)(2,1)} %weight_ref.1), custom_call_target="tpu_custom_call" | custom-call | tf_op jit(solution)/shard_map/pallas_call | solution.py:65
  4.6 11.5 %collective-permute-start.1 = (bf16[1,256,256]{2,1,0:T(8,128)(2,1)S(1)}, bf16[1,256,256]{2,1,0:T(8,128)(2,1)S(1)}, u32[]{:S(2)}, u32[]{:S(2)}) collective-permute-start(bf16[1,256,256]{2,1,0:T(8,128)(2,1)S(1)} %get-tuple-element.9), channel_id=1, source_target_pairs={{0,1},{1,0},{2,3},{3,2},{4,5},{5,4},{6,7},{7,6},{8,15},{9,10},{10,... | collective-permute-start | bytes 393224 | tf_op jit(solution)/shard_map/ppermute | solution.py:174
  16.0 1.9 %collective-permute-start = (bf16[3,256,256]{2,1,0:T(8,128)(2,1)S(1)}, bf16[3,256,256]{2,1,0:T(8,128)(2,1)S(1)}, u32[]{:S(2)}, u32[]{:S(2)}) collective-permute-start(bf16[3,256,256]{2,1,0:T(8,128)(2,1)S(1)} %get-tuple-element.7), channel_id=1, source_target_pairs={{0,1},{1,0},{2,3},{3,2},{4,5},{5,4},{6,7},{7,6},{8,15},{9,10},{10,... | collective-permute-start | bytes 1179656 | tf_op jit(solution)/shard_map/ppermute | solution.py:175
  18.0 0.1 iota_compare_fusion.2
  18.2 0.2 convert_reduce_fusion
  18.4 0.2 reduce_window_sum.11
  18.7 0.3 fusion.15
  19.0 0.1 fusion.10
  19.2 0.1 add.59.slot_ref
  19.4 0.1 select_reduce_fusion
  19.6 4.5 %collective-permute-start.2 = (bf16[256,256]{1,0:T(8,128)(2,1)S(1)}, bf16[256,256]{1,0:T(8,128)(2,1)S(1)}, u32[]{:S(2)}, u32[]{:S(2)}) collective-permute-start(bf16[256,256]{1,0:T(8,128)(2,1)S(1)} %fusion.4), channel_id=1, source_target_pairs={{0,4},{1,5},{2,6},{3,7},{4,0},{5,1},{6,2},{7,3},{8,12},{9,13},{10,... | collective-permute-start | bytes 393224 | tf_op jit(solution)/shard_map/ppermute | solution.py:179
  24.1 3.1 %collective-permute-done = bf16[3,256,256]{2,1,0:T(8,128)(2,1)S(1)} collective-permute-done((bf16[3,256,256]{2,1,0:T(8,128)(2,1)S(1)}, bf16[3,256,256]{2,1,0:T(8,128)(2,1)S(1)}, u32[]{:S(2)}, u32[]{:S(2)}) %collective-permute-start) | collective-permute-done | bytes 393248 | tf_op jit(solution)/shard_map/ppermute | solution.py:175
  27.3 1.9 %collective-permute-start.4 = (bf16[256,256]{1,0:T(8,128)(2,1)S(1)}, bf16[256,256]{1,0:T(8,128)(2,1)S(1)}, u32[]{:S(2)}, u32[]{:S(2)}) collective-permute-start(bf16[256,256]{1,0:T(8,128)(2,1)S(1)} %get-tuple-element.12), channel_id=1, source_target_pairs={{0,6},{1,7},{2,0},{3,1},{4,2},{5,3},{6,4},{7,5},{8,14},{9,15},{10,... | collective-permute-start | bytes 393224 | tf_op jit(solution)/shard_map/ppermute | solution.py:179
  29.2 4.3 %collective-permute-start.3 = (bf16[256,256]{1,0:T(8,128)(2,1)S(1)}, bf16[256,256]{1,0:T(8,128)(2,1)S(1)}, u32[]{:S(2)}, u32[]{:S(2)}) collective-permute-start(bf16[256,256]{1,0:T(8,128)(2,1)S(1)} %get-tuple-element.13), channel_id=1, source_target_pairs={{0,2},{1,3},{2,4},{3,5},{4,6},{5,7},{6,0},{7,1},{8,10},{9,11},{10,... | collective-permute-start | bytes 393224 | tf_op jit(solution)/shard_map/ppermute | solution.py:179
  33.5 4.0 %collective-permute-done.4.c_ref = bf16[256,256]{1,0:T(8,128)(2,1)S(1)} collective-permute-done((bf16[256,256]{1,0:T(8,128)(2,1)S(1)}, bf16[256,256]{1,0:T(8,128)(2,1)S(1)}, u32[]{:S(2)}, u32[]{:S(2)}) %collective-permute-start.4) | collective-permute-done | bytes 131104 | tf_op jit(solution)/shard_map/ppermute | solution.py:179
  37.5 3.3 %collective-permute-done.3.b_ref = bf16[256,256]{1,0:T(8,128)(2,1)S(1)} collective-permute-done((bf16[256,256]{1,0:T(8,128)(2,1)S(1)}, bf16[256,256]{1,0:T(8,128)(2,1)S(1)}, u32[]{:S(2)}, u32[]{:S(2)}) %collective-permute-start.3) | collective-permute-done | bytes 131104 | tf_op jit(solution)/shard_map/ppermute | solution.py:179
  40.8 1.0 %shard_map.105 = bf16[512,256]{1,0:T(8,128)(2,1)} custom-call(s32[1,256]{1,0:T(1,128)S(1)} %add.59.slot_ref, bf16[256,256]{1,0:T(8,128)(2,1)S(1)} %slice_bitcast_fusion.5.kept_ref, bf16[256,256]{1,0:T(8,128)(2,1)S(1)} %slice_bitcast_fusion.4.got_ref, bf16[256,256]{1,0:T(8,128)(2,1)S(1)} %collective-permute-done.2.a_ref, ...), custom_call_target="tpu_custom_call" | custom-call | tf_op jit(solution)/shard_map/pallas_call | solution.py:100
  41.8 12.5 %all-to-all-start = ((bf16[64,8,256]{2,1,0:T(8,128)(2,1)}), bf16[64,8,256]{2,1,0:T(8,128)(2,1)S(1)}, u32[]{:S(2)}, u32[]{:S(2)}) async-start(bf16[64,8,256]{2,1,0:T(8,128)(2,1)} %bitcast.38), calls=%async_computation | async-start | bytes 524288 | tf_op jit(solution)/shard_map/all_to_all | solution.py:198
  54.3 0.1 copy.15
  54.4 0.1 broadcast_in_dim.18
  54.5 0.1 reshape_reshape.4.tag_ref
  54.7 0.8 %fusion.3 = bf16[8,8,128]{2,1,0:T(8,128)(2,1)} fusion(bf16[8,128,1,256]{3,1,0,2:T(8,128)(2,1)S(1)} %bitcast.41, f32[8,8]{1,0:T(8,128)S(1)} %get-tuple-element.15, f32[8,128]{1,0:T(8,128)S(1)} %get-tuple-element.16, f32[8,8]{1,0:T(8,128)S(1)} %get-tuple-element.14, bf16[8,8,128]{2,1,0:T(8,128)(2,1)S(1)} %get-tuple-element.19), kind=kOutput, calls=%fused_computation.5 | convolution fusion | flops 2129920 | bytes 307200 | tf_op jit(solution)/shard_map/bkgs,bskd->bkgd/dot_general | solution.py:222
  55.5 10.8 %all-to-all-done = bf16[64,8,256]{2,1,0:T(8,128)(2,1)S(1)} async-done(((bf16[64,8,256]{2,1,0:T(8,128)(2,1)}), bf16[64,8,256]{2,1,0:T(8,128)(2,1)S(1)}, u32[]{:S(2)}, u32[]{:S(2)}) %all-to-all-start) | async-done | bytes 262176 | tf_op jit(solution)/shard_map/all_to_all | solution.py:198
  66.3 1.0 %shard_map.106 = bf16[8,8,128]{2,1,0:T(8,128)(2,1)} custom-call(s32[1,512]{1,0:T(1,128)S(1)} %reshape_reshape.4.tag_ref, bf16[8,8,128]{2,1,0:T(8,128)(2,1)S(1)} %copy-done.1, bf16[512,256]{1,0:T(8,128)(2,1)S(1)} %bitcast.37), custom_call_target="tpu_custom_call" | custom-call | tf_op jit(solution)/shard_map/pallas_call | solution.py:134
  (30 shorter events, 0.4 us)
Async XLA Ops:
  0.6 18.1 %copy-start = (bf16[8,8,128]{2,1,0:T(8,128)(2,1)S(1)}, bf16[8,8,128]{2,1,0:T(8,128)(2,1)}, u32[]{:S(2)}) copy-start(bf16[8,8,128]{2,1,0:T(8,128)(2,1)} %param.14) | copy-start | bytes 49156
  0.6 17.3 %copy-start.6 = (s32[8]{0:T(128)S(1)}, s32[8]{0:T(128)}, u32[]{:S(2)}) copy-start(s32[8]{0:T(128)} %param.17) | copy-start | bytes 100
  0.7 17.4 %copy-start.4 = (bf16[8,1,256]{2,0,1:T(8,128)(2,1)S(1)}, bf16[8,1,256]{2,0,1:T(8,128)(2,1)}, u32[]{:S(2)}) copy-start(bf16[8,1,256]{2,0,1:T(8,128)(2,1)} %param.16) | copy-start | bytes 12292
  0.7 17.4 %copy-start.2 = (s32[4096]{0:T(1024)S(1)}, s32[4096]{0:T(1024)}, u32[]{:S(2)}) copy-start(s32[4096]{0:T(1024)} %param.11) | copy-start | bytes 49156
  0.7 18.0 %copy-start.5 = (bf16[8,128,1,256]{3,1,2,0:T(8,128)(2,1)S(1)}, bf16[8,128,1,256]{3,1,2,0:T(8,128)(2,1)}, u32[]{:S(2)}) copy-start(bf16[8,128,1,256]{3,1,2,0:T(8,128)(2,1)} %param.15) | copy-start | bytes 1572868
  0.7 18.6 %copy-start.3 = (s32[4096]{0:T(1024)S(1)}, s32[4096]{0:T(1024)}, u32[]{:S(2)}) copy-start(s32[4096]{0:T(1024)} %param.12) | copy-start | bytes 49156
  0.7 65.6 %copy-start.1 = (bf16[8,8,128]{2,1,0:T(8,128)(2,1)S(1)}, bf16[8,8,128]{2,1,0:T(8,128)(2,1)}, u32[]{:S(2)}) copy-start(bf16[8,8,128]{2,1,0:T(8,128)(2,1)} %query_ref.1) | copy-start | bytes 49156
  4.6 15.0 %collective-permute-start.1 = (bf16[1,256,256]{2,1,0:T(8,128)(2,1)S(1)}, bf16[1,256,256]{2,1,0:T(8,128)(2,1)S(1)}, u32[]{:S(2)}, u32[]{:S(2)}) collective-permute-start(bf16[1,256,256]{2,1,0:T(8,128)(2,1)S(1)} %get-tuple-element.9), channel_id=1, source_target_pairs={{0,1},{1,0},{2,3},{3,2},{4,5},{5,4},{6,7},{7,6},{8,15},{9,10},{10,... | collective-permute-start | bytes 393224 | tf_op jit(solution)/shard_map/ppermute | solution.py:174
  16.0 11.1 %collective-permute-start = (bf16[3,256,256]{2,1,0:T(8,128)(2,1)S(1)}, bf16[3,256,256]{2,1,0:T(8,128)(2,1)S(1)}, u32[]{:S(2)}, u32[]{:S(2)}) collective-permute-start(bf16[3,256,256]{2,1,0:T(8,128)(2,1)S(1)} %get-tuple-element.7), channel_id=1, source_target_pairs={{0,1},{1,0},{2,3},{3,2},{4,5},{5,4},{6,7},{7,6},{8,15},{9,10},{10,... | collective-permute-start | bytes 1179656 | tf_op jit(solution)/shard_map/ppermute | solution.py:175
  19.6 13.9 %collective-permute-start.2 = (bf16[256,256]{1,0:T(8,128)(2,1)S(1)}, bf16[256,256]{1,0:T(8,128)(2,1)S(1)}, u32[]{:S(2)}, u32[]{:S(2)}) collective-permute-start(bf16[256,256]{1,0:T(8,128)(2,1)S(1)} %fusion.4), channel_id=1, source_target_pairs={{0,4},{1,5},{2,6},{3,7},{4,0},{5,1},{6,2},{7,3},{8,12},{9,13},{10,... | collective-permute-start | bytes 393224 | tf_op jit(solution)/shard_map/ppermute | solution.py:179
  27.3 10.3 %collective-permute-start.4 = (bf16[256,256]{1,0:T(8,128)(2,1)S(1)}, bf16[256,256]{1,0:T(8,128)(2,1)S(1)}, u32[]{:S(2)}, u32[]{:S(2)}) collective-permute-start(bf16[256,256]{1,0:T(8,128)(2,1)S(1)} %get-tuple-element.12), channel_id=1, source_target_pairs={{0,6},{1,7},{2,0},{3,1},{4,2},{5,3},{6,4},{7,5},{8,14},{9,15},{10,... | collective-permute-start | bytes 393224 | tf_op jit(solution)/shard_map/ppermute | solution.py:179
  29.2 11.6 %collective-permute-start.3 = (bf16[256,256]{1,0:T(8,128)(2,1)S(1)}, bf16[256,256]{1,0:T(8,128)(2,1)S(1)}, u32[]{:S(2)}, u32[]{:S(2)}) collective-permute-start(bf16[256,256]{1,0:T(8,128)(2,1)S(1)} %get-tuple-element.13), channel_id=1, source_target_pairs={{0,2},{1,3},{2,4},{3,5},{4,6},{5,7},{6,0},{7,1},{8,10},{9,11},{10,... | collective-permute-start | bytes 393224 | tf_op jit(solution)/shard_map/ppermute | solution.py:179
  41.8 24.4 %all-to-all-start = ((bf16[64,8,256]{2,1,0:T(8,128)(2,1)}), bf16[64,8,256]{2,1,0:T(8,128)(2,1)S(1)}, u32[]{:S(2)}, u32[]{:S(2)}) async-start(bf16[64,8,256]{2,1,0:T(8,128)(2,1)} %bitcast.38), calls=%async_computation | async-start | bytes 524288 | tf_op jit(solution)/shard_map/all_to_all | solution.py:198
where the time goes:
time: 67.6 us; the launch traced here: 67.3 us
  starting transfers between devices  36.6 us (54%)
  waiting for transfers between devices  21.2 us (31%)
  Pallas kernels  5.88 us (9%)
  matrix products  1.25 us (2%)
  between operations  0.88 us (1%)
  other arithmetic  0.85 us (1%)
    all_to_all x1, starting transfers between devices, local(): lax.all_to_all(outgoing, 'replica', split_axis=0, concat_axis=0, tiled=True)  12.5 us
    ppermute x1, starting transfers between devices, local(): got_a = lax.ppermute(sent_a, both, neighbours)  11.5 us
    all_to_all x1, waiting for transfers between devices, local(): lax.all_to_all(outgoing, 'replica', split_axis=0, concat_axis=0, tiled=True)  10.8 us
    ppermute x3, starting transfers between devices, onward(): lax.ppermute(outward, 'tensor', [(z, (z + 2 * step) % n_ten) for z in ran...  10.7 us
    ppermute x3, waiting for transfers between devices, onward(): lax.ppermute(outward, 'tensor', [(z, (z + 2 * step) % n_ten) for z in ran...  7.34 us
    pallas_call x1, Pallas kernels, project(): pl.pallas_call(project_body, in_specs=[pl.BlockSpec(memory_space=pltpu.HB...  3.84 us
    ppermute x1, waiting for transfers between devices, local(): got_b = lax.ppermute(sent_b, both, neighbours)  3.07 us
    ppermute x1, starting transfers between devices, local(): got_b = lax.ppermute(sent_b, both, neighbours)  1.92 us
  transfers between devices with their start and end apart: 6, of which 4 were waited for; matrix products, arithmetic and copies ran while one was open for 4% of the time, Pallas kernels for 0%

commit v1 on v0

--- a/solution.py
+++ b/solution.py
@@ -173,6 +173,20 @@
     sent_a, sent_b, kept_a, kept_b = project(features, kv_weight)
     got_a = lax.ppermute(sent_a, both, neighbours)
     got_b = lax.ppermute(sent_b, both, neighbours)
+    *later, got_b = lax.optimization_barrier(
+        (
+            image_owner,
+            image_request,
+            cross_query,
+            self_query,
+            self_cache,
+            fresh_key_value,
+            cache_len,
+            got_b,
+        )
+    )
+    image_owner, image_request, cross_query, self_query, *later = later
+    self_cache, fresh_key_value, cache_len = later
 
     def onward(kept, got, step):
         outward = (kept.astype(jnp.float32) + got.astype(jnp.float32)).astype(jnp.bfloat16)

time: 67.6 us -> 68.2 us (level)
    ppermute x3, waiting for transfers between devices: 7.34 us -> 4.08 us  [onward(): lax.ppermute(outward, 'tensor', [(z, (z + 2 * step) % n_ten) for z in ran...]
    ppermute x1, waiting for transfers between devices: 3.07 us -> 6.06 us  [local(): got_b = lax.ppermute(sent_b, both, neighbours)]
  transfers between devices with their start and end apart: 6 -> 6, of which waited for: 4 -> 5; matrix products, arithmetic and copies ran while one was open for 4% -> 4% of each run, Pallas kernels for 0% -> 0%
where the time goes in v1:
time: 68.2 us; the launch traced here: 67.9 us
  starting transfers between devices  37.1 us (54%)
  waiting for transfers between devices  21.3 us (31%)
  Pallas kernels  5.89 us (9%)
  matrix products  1.25 us (2%)
  between operations  0.87 us (1%)
  other arithmetic  0.84 us (1%)
    all_to_all x1, starting transfers between devices, local(): lax.all_to_all(outgoing, 'replica', split_axis=0, concat_axis=0, tiled=True)  12.9 us
    ppermute x1, starting transfers between devices, local(): got_a = lax.ppermute(sent_a, both, neighbours)  11.5 us
    all_to_all x1, waiting for transfers between devices, local(): lax.all_to_all(outgoing, 'replica', split_axis=0, concat_axis=0, tiled=True)  10.8 us
    ppermute x3, starting transfers between devices, onward(): lax.ppermute(outward, 'tensor', [(z, (z + 2 * step) % n_ten) for z in ran...  10.7 us
    ppermute x1, waiting for transfers between devices, local(): got_b = lax.ppermute(sent_b, both, neighbours)  6.06 us
    ppermute x3, waiting for transfers between devices, onward(): lax.ppermute(outward, 'tensor', [(z, (z + 2 * step) % n_ten) for z in ran...  4.08 us
    pallas_call x1, Pallas kernels, project(): pl.pallas_call(project_body, in_specs=[pl.BlockSpec(memory_space=pltpu.HB...  3.85 us
    ppermute x1, starting transfers between devices, local(): got_b = lax.ppermute(sent_b, both, neighbours)  1.92 us
  transfers between devices with their start and end apart: 6, of which 5 were waited for; matrix products, arithmetic and copies ran while one was open for 4% of the time, Pallas kernels for 0%

profile of v1, /device:TPU:1, one launch (start us, length us, event | category | flops | bytes accessed | tf_op | source)
XLA Modules:
  0.0 67.9 jit_solution(18200539533835714654)
XLA Ops:
  0.7 3.8 %shard_map.104 = (bf16[1,256,256]{2,1,0:T(8,128)(2,1)S(1)}, bf16[3,256,256]{2,1,0:T(8,128)(2,1)S(1)}, bf16[1,256,256]{2,1,0:T(8,128)(2,1)S(1)}, bf16[3,256,256]{2,1,0:T(8,128)(2,1)S(1)}) custom-call(bf16[64,4,960]{2,1,0:T(4,128)(2,1)} %features_ref.1, bf16[960,8,256]{2,1,0:T(8,128)(2,1)} %weight_ref.1), custom_call_target="tpu_custom_call" | custom-call | tf_op jit(solution)/shard_map/pallas_call | solution.py:65
  4.6 11.5 %collective-permute-start.1 = (bf16[1,256,256]{2,1,0:T(8,128)(2,1)S(1)}, bf16[1,256,256]{2,1,0:T(8,128)(2,1)S(1)}, u32[]{:S(2)}, u32[]{:S(2)}) collective-permute-start(bf16[1,256,256]{2,1,0:T(8,128)(2,1)S(1)} %get-tuple-element.21), channel_id=1, source_target_pairs={{0,1},{1,0},{2,3},{3,2},{4,5},{5,4},{6,7},{7,6},{8,15},{9,10},{10,... | collective-permute-start | bytes 393224 | tf_op jit(solution)/shard_map/ppermute | solution.py:174
  16.1 1.9 %collective-permute-start = (bf16[3,256,256]{2,1,0:T(8,128)(2,1)S(1)}, bf16[3,256,256]{2,1,0:T(8,128)(2,1)S(1)}, u32[]{:S(2)}, u32[]{:S(2)}) collective-permute-start(bf16[3,256,256]{2,1,0:T(8,128)(2,1)S(1)} %get-tuple-element.14), channel_id=1, source_target_pairs={{0,1},{1,0},{2,3},{3,2},{4,5},{5,4},{6,7},{7,6},{8,15},{9,10},{10,... | collective-permute-start | bytes 1179656 | tf_op jit(solution)/shard_map/ppermute | solution.py:175
  18.0 0.4 collective-permute-done.1
  18.4 4.5 %collective-permute-start.2 = (bf16[256,256]{1,0:T(8,128)(2,1)S(1)}, bf16[256,256]{1,0:T(8,128)(2,1)S(1)}, u32[]{:S(2)}, u32[]{:S(2)}) collective-permute-start(bf16[256,256]{1,0:T(8,128)(2,1)S(1)} %fusion.4), channel_id=1, source_target_pairs={{0,4},{1,5},{2,6},{3,7},{4,0},{5,1},{6,2},{7,3},{8,12},{9,13},{10,... | collective-permute-start | bytes 393224 | tf_op jit(solution)/shard_map/ppermute | solution.py:193
  23.0 6.1 %collective-permute-done = bf16[3,256,256]{2,1,0:T(8,128)(2,1)S(1)} collective-permute-done((bf16[3,256,256]{2,1,0:T(8,128)(2,1)S(1)}, bf16[3,256,256]{2,1,0:T(8,128)(2,1)S(1)}, u32[]{:S(2)}, u32[]{:S(2)}) %collective-permute-start) | collective-permute-done | bytes 393248 | tf_op jit(solution)/shard_map/ppermute | solution.py:175
  29.3 0.2 convert_reduce_fusion
  29.6 0.2 reduce_window_sum.11
  29.8 1.9 %collective-permute-start.4 = (bf16[256,256]{1,0:T(8,128)(2,1)S(1)}, bf16[256,256]{1,0:T(8,128)(2,1)S(1)}, u32[]{:S(2)}, u32[]{:S(2)}) collective-permute-start(bf16[256,256]{1,0:T(8,128)(2,1)S(1)} %get-tuple-element.28), channel_id=1, source_target_pairs={{0,6},{1,7},{2,0},{3,1},{4,2},{5,3},{6,4},{7,5},{8,14},{9,15},{10,... | collective-permute-start | bytes 393224 | tf_op jit(solution)/shard_map/ppermute | solution.py:193
  31.8 4.3 %collective-permute-start.3 = (bf16[256,256]{1,0:T(8,128)(2,1)S(1)}, bf16[256,256]{1,0:T(8,128)(2,1)S(1)}, u32[]{:S(2)}, u32[]{:S(2)}) collective-permute-start(bf16[256,256]{1,0:T(8,128)(2,1)S(1)} %get-tuple-element.29), channel_id=1, source_target_pairs={{0,2},{1,3},{2,4},{3,5},{4,6},{5,7},{6,0},{7,1},{8,10},{9,11},{10,... | collective-permute-start | bytes 393224 | tf_op jit(solution)/shard_map/ppermute | solution.py:193
  36.0 0.3 fusion.15
  36.4 0.1 fusion.10
  36.5 0.1 add.59.slot_ref
  36.7 0.1 select_reduce_fusion
  36.9 0.3 collective-permute-done.4.c_ref
  37.2 3.7 %collective-permute-done.3.b_ref = bf16[256,256]{1,0:T(8,128)(2,1)S(1)} collective-permute-done((bf16[256,256]{1,0:T(8,128)(2,1)S(1)}, bf16[256,256]{1,0:T(8,128)(2,1)S(1)}, u32[]{:S(2)}, u32[]{:S(2)}) %collective-permute-start.3) | collective-permute-done | bytes 131104 | tf_op jit(solution)/shard_map/ppermute | solution.py:193
  40.9 1.0 %shard_map.105 = bf16[512,256]{1,0:T(8,128)(2,1)} custom-call(s32[1,256]{1,0:T(1,128)S(1)} %add.59.slot_ref, bf16[256,256]{1,0:T(8,128)(2,1)S(1)} %slice_bitcast_fusion.5.kept_ref, bf16[256,256]{1,0:T(8,128)(2,1)S(1)} %slice_bitcast_fusion.4.got_ref, bf16[256,256]{1,0:T(8,128)(2,1)S(1)} %collective-permute-done.2.a_ref, ...), custom_call_target="tpu_custom_call" | custom-call | tf_op jit(solution)/shard_map/pallas_call | solution.py:100
  41.9 12.9 %all-to-all-start = ((bf16[64,8,256]{2,1,0:T(8,128)(2,1)}), bf16[64,8,256]{2,1,0:T(8,128)(2,1)S(1)}, u32[]{:S(2)}, u32[]{:S(2)}) async-start(bf16[64,8,256]{2,1,0:T(8,128)(2,1)} %bitcast.38), calls=%async_computation | async-start | bytes 524288 | tf_op jit(solution)/shard_map/all_to_all | solution.py:212
  54.9 0.1 copy.15
  55.0 0.1 broadcast_in_dim.18
  55.1 0.1 reshape_reshape.4.tag_ref
  55.3 0.8 %fusion.3 = bf16[8,8,128]{2,1,0:T(8,128)(2,1)} fusion(bf16[8,128,1,256]{3,1,0,2:T(8,128)(2,1)S(1)} %bitcast.41, f32[8,8]{1,0:T(8,128)S(1)} %get-tuple-element.31, f32[8,128]{1,0:T(8,128)S(1)} %get-tuple-element.32, f32[8,8]{1,0:T(8,128)S(1)} %get-tuple-element.30, bf16[8,8,128]{2,1,0:T(8,128)(2,1)S(1)} %get-tuple-element.35), kind=kOutput, calls=%fused_computation.5 | convolution fusion | flops 2129920 | bytes 307200 | tf_op jit(solution)/shard_map/bkgs,bskd->bkgd/dot_general | solution.py:236
  56.1 10.8 %all-to-all-done = bf16[64,8,256]{2,1,0:T(8,128)(2,1)S(1)} async-done(((bf16[64,8,256]{2,1,0:T(8,128)(2,1)}), bf16[64,8,256]{2,1,0:T(8,128)(2,1)S(1)}, u32[]{:S(2)}, u32[]{:S(2)}) %all-to-all-start) | async-done | bytes 262176 | tf_op jit(solution)/shard_map/all_to_all | solution.py:212
  66.9 1.0 %shard_map.106 = bf16[8,8,128]{2,1,0:T(8,128)(2,1)} custom-call(s32[1,512]{1,0:T(1,128)S(1)} %reshape_reshape.4.tag_ref, bf16[8,8,128]{2,1,0:T(8,128)(2,1)S(1)} %copy-done.1, bf16[512,256]{1,0:T(8,128)(2,1)S(1)} %bitcast.37), custom_call_target="tpu_custom_call" | custom-call | tf_op jit(solution)/shard_map/pallas_call | solution.py:134
  (30 shorter events, 0.5 us)
Async XLA Ops:
  0.6 35.4 %copy-start = (bf16[8,8,128]{2,1,0:T(8,128)(2,1)S(1)}, bf16[8,8,128]{2,1,0:T(8,128)(2,1)}, u32[]{:S(2)}) copy-start(bf16[8,8,128]{2,1,0:T(8,128)(2,1)} %param.14) | copy-start | bytes 49156
  0.6 28.5 %copy-start.6 = (s32[8]{0:T(128)S(1)}, s32[8]{0:T(128)}, u32[]{:S(2)}) copy-start(s32[8]{0:T(128)} %param.17) | copy-start | bytes 100
  0.7 28.6 %copy-start.4 = (bf16[8,1,256]{2,0,1:T(8,128)(2,1)S(1)}, bf16[8,1,256]{2,0,1:T(8,128)(2,1)}, u32[]{:S(2)}) copy-start(bf16[8,1,256]{2,0,1:T(8,128)(2,1)} %param.16) | copy-start | bytes 12292
  0.7 35.4 %copy-start.5 = (bf16[8,128,1,256]{3,1,2,0:T(8,128)(2,1)S(1)}, bf16[8,128,1,256]{3,1,2,0:T(8,128)(2,1)}, u32[]{:S(2)}) copy-start(bf16[8,128,1,256]{3,1,2,0:T(8,128)(2,1)} %param.15) | copy-start | bytes 1572868
  0.7 66.2 %copy-start.1 = (bf16[8,8,128]{2,1,0:T(8,128)(2,1)S(1)}, bf16[8,8,128]{2,1,0:T(8,128)(2,1)}, u32[]{:S(2)}) copy-start(bf16[8,8,128]{2,1,0:T(8,128)(2,1)} %query_ref) | copy-start | bytes 49156
  0.7 35.9 %copy-start.3 = (s32[4096]{0:T(1024)S(1)}, s32[4096]{0:T(1024)}, u32[]{:S(2)}) copy-start(s32[4096]{0:T(1024)} %param.12) | copy-start | bytes 49156
  0.7 28.5 %copy-start.2 = (s32[4096]{0:T(1024)S(1)}, s32[4096]{0:T(1024)}, u32[]{:S(2)}) copy-start(s32[4096]{0:T(1024)} %param.11) | copy-start | bytes 49156
  4.6 13.8 %collective-permute-start.1 = (bf16[1,256,256]{2,1,0:T(8,128)(2,1)S(1)}, bf16[1,256,256]{2,1,0:T(8,128)(2,1)S(1)}, u32[]{:S(2)}, u32[]{:S(2)}) collective-permute-start(bf16[1,256,256]{2,1,0:T(8,128)(2,1)S(1)} %get-tuple-element.21), channel_id=1, source_target_pairs={{0,1},{1,0},{2,3},{3,2},{4,5},{5,4},{6,7},{7,6},{8,15},{9,10},{10,... | collective-permute-start | bytes 393224 | tf_op jit(solution)/shard_map/ppermute | solution.py:174
  16.1 13.0 %collective-permute-start = (bf16[3,256,256]{2,1,0:T(8,128)(2,1)S(1)}, bf16[3,256,256]{2,1,0:T(8,128)(2,1)S(1)}, u32[]{:S(2)}, u32[]{:S(2)}) collective-permute-start(bf16[3,256,256]{2,1,0:T(8,128)(2,1)S(1)} %get-tuple-element.14), channel_id=1, source_target_pairs={{0,1},{1,0},{2,3},{3,2},{4,5},{5,4},{6,7},{7,6},{8,15},{9,10},{10,... | collective-permute-start | bytes 1179656 | tf_op jit(solution)/shard_map/ppermute | solution.py:175
  18.4 18.4 %collective-permute-start.2 = (bf16[256,256]{1,0:T(8,128)(2,1)S(1)}, bf16[256,256]{1,0:T(8,128)(2,1)S(1)}, u32[]{:S(2)}, u32[]{:S(2)}) collective-permute-start(bf16[256,256]{1,0:T(8,128)(2,1)S(1)} %fusion.4), channel_id=1, source_target_pairs={{0,4},{1,5},{2,6},{3,7},{4,0},{5,1},{6,2},{7,3},{8,12},{9,13},{10,... | collective-permute-start | bytes 393224 | tf_op jit(solution)/shard_map/ppermute | solution.py:193
  29.8 7.3 %collective-permute-start.4 = (bf16[256,256]{1,0:T(8,128)(2,1)S(1)}, bf16[256,256]{1,0:T(8,128)(2,1)S(1)}, u32[]{:S(2)}, u32[]{:S(2)}) collective-permute-start(bf16[256,256]{1,0:T(8,128)(2,1)S(1)} %get-tuple-element.28), channel_id=1, source_target_pairs={{0,6},{1,7},{2,0},{3,1},{4,2},{5,3},{6,4},{7,5},{8,14},{9,15},{10,... | collective-permute-start | bytes 393224 | tf_op jit(solution)/shard_map/ppermute | solution.py:193
  31.8 9.2 %collective-permute-start.3 = (bf16[256,256]{1,0:T(8,128)(2,1)S(1)}, bf16[256,256]{1,0:T(8,128)(2,1)S(1)}, u32[]{:S(2)}, u32[]{:S(2)}) collective-permute-start(bf16[256,256]{1,0:T(8,128)(2,1)S(1)} %get-tuple-element.29), channel_id=1, source_target_pairs={{0,2},{1,3},{2,4},{3,5},{4,6},{5,7},{6,0},{7,1},{8,10},{9,11},{10,... | collective-permute-start | bytes 393224 | tf_op jit(solution)/shard_map/ppermute | solution.py:193
  41.9 24.9 %all-to-all-start = ((bf16[64,8,256]{2,1,0:T(8,128)(2,1)}), bf16[64,8,256]{2,1,0:T(8,128)(2,1)S(1)}, u32[]{:S(2)}, u32[]{:S(2)}) async-start(bf16[64,8,256]{2,1,0:T(8,128)(2,1)} %bitcast.38), calls=%async_computation | async-start | bytes 524288 | tf_op jit(solution)/shard_map/all_to_all | solution.py:212

commit v2 on v0

--- a/solution.py
+++ b/solution.py
@@ -60,7 +60,7 @@
     images, patches, block = features.shape
     heads, width = weight.shape[1:]
     rows = images * patches
-    counts = (1, heads // 2 - 1) * 2
+    counts = (heads // 4,) * 4
     copies = pl.cdiv(block, STEP)
     return pl.pallas_call(
         project_body,
@@ -180,8 +180,8 @@
 
     arrivals = (
         onward(kept_a[0], got_a[0], 2),
-        onward(kept_b[0], got_b[0], 1),
-        onward(kept_b[1], got_b[1], quarter - 1),
+        onward(kept_a[1], got_a[1], 1),
+        onward(kept_b[0], got_b[0], quarter - 1),
     )
 
     owners = image_owner.reshape(n_rep, images)
@@ -193,7 +193,7 @@
     rank = jnp.sum((same_owner & earlier).astype(jnp.int32), axis=1, dtype=jnp.int32)
     slot = own_block * slot_cap + rank
     row_slot = (slot[:, None] * patches + jnp.arange(patches, dtype=jnp.int32)[None, :]).reshape(rows)
-    outgoing = place(row_slot, kept_b[2], got_b[2], arrivals, slot_all * patches)
+    outgoing = place(row_slot, kept_b[1], got_b[1], arrivals, slot_all * patches)
     outgoing = outgoing.reshape(n_rep, slot_cap * patches, width2)
     arrived = lax.all_to_all(outgoing, "replica", split_axis=0, concat_axis=0, tiled=True)
 

time: 67.6 us -> 65 us (0.962)
  starting transfers between devices: 36.6 us -> 34.4 us
    ppermute x1, starting transfers between devices: 11.5 us -> 1.92 us  [local(): got_a = lax.ppermute(sent_a, both, neighbours)]
    ppermute x1, starting transfers between devices: 1.92 us -> 11.5 us  [local(): got_b = lax.ppermute(sent_b, both, neighbours)]
    ppermute x1, waiting for transfers between devices: 3.07 us -> 0.28 us  [local(): got_b = lax.ppermute(sent_b, both, neighbours)]
    ppermute x3, waiting for transfers between devices: 7.34 us -> 8.87 us  [onward(): lax.ppermute(outward, 'tensor', [(z, (z + 2 * step) % n_ten) for z in ran...]
    all_to_all x1, starting transfers between devices: 12.5 us -> 11.1 us  [local(): lax.all_to_all(outgoing, 'replica', split_axis=0, concat_axis=0, tiled=True)]
    ppermute x1, waiting for transfers between devices: 0.01 us -> 0.89 us  [local(): got_a = lax.ppermute(sent_a, both, neighbours)]
    ppermute x3, starting transfers between devices: 10.7 us -> 9.85 us  [onward(): lax.ppermute(outward, 'tensor', [(z, (z + 2 * step) % n_ten) for z in ran...]
  transfers between devices with their start and end apart: 6 -> 6, of which waited for: 4 -> 5; matrix products, arithmetic and copies ran while one was open for 4% -> 4% of each run, Pallas kernels for 0% -> 0%
where the time goes in v2:
time: 65 us; the launch traced here: 64.7 us
  starting transfers between devices  34.4 us (53%)
  waiting for transfers between devices  20.8 us (32%)
  Pallas kernels  5.88 us (9%)
  matrix products  1.25 us (2%)
  between operations  0.86 us (1%)
  other arithmetic  0.85 us (1%)
  local copies, waits for them, and re-layouts  0.67 us (1%)
    ppermute x1, starting transfers between devices, local(): got_b = lax.ppermute(sent_b, both, neighbours)  11.5 us
    all_to_all x1, starting transfers between devices, local(): lax.all_to_all(outgoing, 'replica', split_axis=0, concat_axis=0, tiled=True)  11.1 us
    all_to_all x1, waiting for transfers between devices, local(): lax.all_to_all(outgoing, 'replica', split_axis=0, concat_axis=0, tiled=True)  10.8 us
    ppermute x3, starting transfers between devices, onward(): lax.ppermute(outward, 'tensor', [(z, (z + 2 * step) % n_ten) for z in ran...  9.85 us
    ppermute x3, waiting for transfers between devices, onward(): lax.ppermute(outward, 'tensor', [(z, (z + 2 * step) % n_ten) for z in ran...  8.87 us
    pallas_call x1, Pallas kernels, project(): pl.pallas_call(project_body, in_specs=[pl.BlockSpec(memory_space=pltpu.HB...  3.84 us
    ppermute x1, starting transfers between devices, local(): got_a = lax.ppermute(sent_a, both, neighbours)  1.92 us
  transfers between devices with their start and end apart: 6, of which 5 were waited for; matrix products, arithmetic and copies ran while one was open for 4% of the time, Pallas kernels for 0%

profile of v2, /device:TPU:1, one launch (start us, length us, event | category | flops | bytes accessed | tf_op | source)
XLA Modules:
  0.0 64.7 jit_solution(2290334436406125300)
XLA Ops:
  0.7 3.8 %shard_map.104 = (bf16[2,256,256]{2,1,0:T(8,128)(2,1)S(1)}, bf16[2,256,256]{2,1,0:T(8,128)(2,1)S(1)}, bf16[2,256,256]{2,1,0:T(8,128)(2,1)S(1)}, bf16[2,256,256]{2,1,0:T(8,128)(2,1)S(1)}) custom-call(bf16[64,4,960]{2,1,0:T(4,128)(2,1)} %features_ref.1, bf16[960,8,256]{2,1,0:T(8,128)(2,1)} %weight_ref.1), custom_call_target="tpu_custom_call" | custom-call | tf_op jit(solution)/shard_map/pallas_call | solution.py:65
  4.6 11.5 %collective-permute-start = (bf16[2,256,256]{2,1,0:T(8,128)(2,1)S(1)}, bf16[2,256,256]{2,1,0:T(8,128)(2,1)S(1)}, u32[]{:S(2)}, u32[]{:S(2)}) collective-permute-start(bf16[2,256,256]{2,1,0:T(8,128)(2,1)S(1)} %get-tuple-element.7), channel_id=1, source_target_pairs={{0,1},{1,0},{2,3},{3,2},{4,5},{5,4},{6,7},{7,6},{8,15},{9,10},{10,... | collective-permute-start | bytes 786440 | tf_op jit(solution)/shard_map/ppermute | solution.py:175
  16.0 1.9 %collective-permute-start.1 = (bf16[2,256,256]{2,1,0:T(8,128)(2,1)S(1)}, bf16[2,256,256]{2,1,0:T(8,128)(2,1)S(1)}, u32[]{:S(2)}, u32[]{:S(2)}) collective-permute-start(bf16[2,256,256]{2,1,0:T(8,128)(2,1)S(1)} %get-tuple-element.9), channel_id=1, source_target_pairs={{0,1},{1,0},{2,3},{3,2},{4,5},{5,4},{6,7},{7,6},{8,15},{9,10},{10,... | collective-permute-start | bytes 786440 | tf_op jit(solution)/shard_map/ppermute | solution.py:174
  18.2 0.2 convert_reduce_fusion
  18.4 0.2 reduce_window_sum.11
  18.8 0.3 fusion.15
  19.1 0.1 fusion.10
  19.2 0.1 select_reduce_fusion
  19.4 0.1 add.59.slot_ref
  19.5 0.3 collective-permute-done
  19.8 3.6 %collective-permute-start.4 = (bf16[256,256]{1,0:T(8,128)(2,1)S(1)}, bf16[256,256]{1,0:T(8,128)(2,1)S(1)}, u32[]{:S(2)}, u32[]{:S(2)}) collective-permute-start(bf16[256,256]{1,0:T(8,128)(2,1)S(1)} %fusion.6), channel_id=1, source_target_pairs={{0,6},{1,7},{2,0},{3,1},{4,2},{5,3},{6,4},{7,5},{8,14},{9,15},{10,... | collective-permute-start | bytes 393224 | tf_op jit(solution)/shard_map/ppermute | solution.py:179
  23.5 0.9 %collective-permute-done.1 = bf16[2,256,256]{2,1,0:T(8,128)(2,1)S(1)} collective-permute-done((bf16[2,256,256]{2,1,0:T(8,128)(2,1)S(1)}, bf16[2,256,256]{2,1,0:T(8,128)(2,1)S(1)}, u32[]{:S(2)}, u32[]{:S(2)}) %collective-permute-start.1) | collective-permute-done | bytes 262176 | tf_op jit(solution)/shard_map/ppermute | solution.py:174
  24.4 1.9 %collective-permute-start.3 = (bf16[256,256]{1,0:T(8,128)(2,1)S(1)}, bf16[256,256]{1,0:T(8,128)(2,1)S(1)}, u32[]{:S(2)}, u32[]{:S(2)}) collective-permute-start(bf16[256,256]{1,0:T(8,128)(2,1)S(1)} %get-tuple-element.12), channel_id=1, source_target_pairs={{0,2},{1,3},{2,4},{3,5},{4,6},{5,7},{6,0},{7,1},{8,10},{9,11},{10,... | collective-permute-start | bytes 393224 | tf_op jit(solution)/shard_map/ppermute | solution.py:179
  26.4 4.3 %collective-permute-start.2 = (bf16[256,256]{1,0:T(8,128)(2,1)S(1)}, bf16[256,256]{1,0:T(8,128)(2,1)S(1)}, u32[]{:S(2)}, u32[]{:S(2)}) collective-permute-start(bf16[256,256]{1,0:T(8,128)(2,1)S(1)} %get-tuple-element.13), channel_id=1, source_target_pairs={{0,4},{1,5},{2,6},{3,7},{4,0},{5,1},{6,2},{7,3},{8,12},{9,13},{10,... | collective-permute-start | bytes 393224 | tf_op jit(solution)/shard_map/ppermute | solution.py:179
  30.7 5.5 %collective-permute-done.3.b_ref = bf16[256,256]{1,0:T(8,128)(2,1)S(1)} collective-permute-done((bf16[256,256]{1,0:T(8,128)(2,1)S(1)}, bf16[256,256]{1,0:T(8,128)(2,1)S(1)}, u32[]{:S(2)}, u32[]{:S(2)}) %collective-permute-start.3) | collective-permute-done | bytes 131104 | tf_op jit(solution)/shard_map/ppermute | solution.py:179
  36.2 3.4 %collective-permute-done.2.a_ref = bf16[256,256]{1,0:T(8,128)(2,1)S(1)} collective-permute-done((bf16[256,256]{1,0:T(8,128)(2,1)S(1)}, bf16[256,256]{1,0:T(8,128)(2,1)S(1)}, u32[]{:S(2)}, u32[]{:S(2)}) %collective-permute-start.2) | collective-permute-done | bytes 131104 | tf_op jit(solution)/shard_map/ppermute | solution.py:179
  39.6 1.0 %shard_map.105 = bf16[512,256]{1,0:T(8,128)(2,1)} custom-call(s32[1,256]{1,0:T(1,128)S(1)} %add.59.slot_ref, bf16[256,256]{1,0:T(8,128)(2,1)S(1)} %slice_bitcast_fusion.5.kept_ref, bf16[256,256]{1,0:T(8,128)(2,1)S(1)} %slice_bitcast_fusion.4.got_ref, bf16[256,256]{1,0:T(8,128)(2,1)S(1)} %collective-permute-done.2.a_ref, ...), custom_call_target="tpu_custom_call" | custom-call | tf_op jit(solution)/shard_map/pallas_call | solution.py:100
  40.6 11.1 %all-to-all-start = ((bf16[64,8,256]{2,1,0:T(8,128)(2,1)}), bf16[64,8,256]{2,1,0:T(8,128)(2,1)S(1)}, u32[]{:S(2)}, u32[]{:S(2)}) async-start(bf16[64,8,256]{2,1,0:T(8,128)(2,1)} %bitcast.38), calls=%async_computation | async-start | bytes 524288 | tf_op jit(solution)/shard_map/all_to_all | solution.py:198
  51.7 0.1 copy.15
  51.8 0.1 broadcast_in_dim.18
  51.9 0.1 reshape_reshape.4.tag_ref
  52.1 0.8 %fusion.3 = bf16[8,8,128]{2,1,0:T(8,128)(2,1)} fusion(bf16[8,128,1,256]{3,1,0,2:T(8,128)(2,1)S(1)} %bitcast.41, f32[8,8]{1,0:T(8,128)S(1)} %get-tuple-element.15, f32[8,128]{1,0:T(8,128)S(1)} %get-tuple-element.16, f32[8,8]{1,0:T(8,128)S(1)} %get-tuple-element.14, bf16[8,8,128]{2,1,0:T(8,128)(2,1)S(1)} %get-tuple-element.19), kind=kOutput, calls=%fused_computation.5 | convolution fusion | flops 2129920 | bytes 307200 | tf_op jit(solution)/shard_map/bkgs,bskd->bkgd/dot_general | solution.py:222
  52.9 10.8 %all-to-all-done = bf16[64,8,256]{2,1,0:T(8,128)(2,1)S(1)} async-done(((bf16[64,8,256]{2,1,0:T(8,128)(2,1)}), bf16[64,8,256]{2,1,0:T(8,128)(2,1)S(1)}, u32[]{:S(2)}, u32[]{:S(2)}) %all-to-all-start) | async-done | bytes 262176 | tf_op jit(solution)/shard_map/all_to_all | solution.py:198
  63.6 1.0 %shard_map.106 = bf16[8,8,128]{2,1,0:T(8,128)(2,1)} custom-call(s32[1,512]{1,0:T(1,128)S(1)} %reshape_reshape.4.tag_ref, bf16[8,8,128]{2,1,0:T(8,128)(2,1)S(1)} %copy-done.1, bf16[512,256]{1,0:T(8,128)(2,1)S(1)} %bitcast.37), custom_call_target="tpu_custom_call" | custom-call | tf_op jit(solution)/shard_map/pallas_call | solution.py:134
  (30 shorter events, 0.5 us)
Async XLA Ops:
  0.6 18.1 %copy-start = (bf16[8,8,128]{2,1,0:T(8,128)(2,1)S(1)}, bf16[8,8,128]{2,1,0:T(8,128)(2,1)}, u32[]{:S(2)}) copy-start(bf16[8,8,128]{2,1,0:T(8,128)(2,1)} %param.14) | copy-start | bytes 49156
  0.6 17.3 %copy-start.6 = (s32[8]{0:T(128)S(1)}, s32[8]{0:T(128)}, u32[]{:S(2)}) copy-start(s32[8]{0:T(128)} %param.17) | copy-start | bytes 100
  0.7 17.4 %copy-start.4 = (bf16[8,1,256]{2,0,1:T(8,128)(2,1)S(1)}, bf16[8,1,256]{2,0,1:T(8,128)(2,1)}, u32[]{:S(2)}) copy-start(bf16[8,1,256]{2,0,1:T(8,128)(2,1)} %param.16) | copy-start | bytes 12292
  0.7 17.4 %copy-start.2 = (s32[4096]{0:T(1024)S(1)}, s32[4096]{0:T(1024)}, u32[]{:S(2)}) copy-start(s32[4096]{0:T(1024)} %param.11) | copy-start | bytes 49156
  0.7 18.0 %copy-start.3 = (s32[4096]{0:T(1024)S(1)}, s32[4096]{0:T(1024)}, u32[]{:S(2)}) copy-start(s32[4096]{0:T(1024)} %param.12) | copy-start | bytes 49156
  0.7 18.1 %copy-start.5 = (bf16[8,128,1,256]{3,1,2,0:T(8,128)(2,1)S(1)}, bf16[8,128,1,256]{3,1,2,0:T(8,128)(2,1)}, u32[]{:S(2)}) copy-start(bf16[8,128,1,256]{3,1,2,0:T(8,128)(2,1)} %param.15) | copy-start | bytes 1572868
  0.7 62.9 %copy-start.1 = (bf16[8,8,128]{2,1,0:T(8,128)(2,1)S(1)}, bf16[8,8,128]{2,1,0:T(8,128)(2,1)}, u32[]{:S(2)}) copy-start(bf16[8,8,128]{2,1,0:T(8,128)(2,1)} %query_ref.1) | copy-start | bytes 49156
  4.6 15.2 %collective-permute-start = (bf16[2,256,256]{2,1,0:T(8,128)(2,1)S(1)}, bf16[2,256,256]{2,1,0:T(8,128)(2,1)S(1)}, u32[]{:S(2)}, u32[]{:S(2)}) collective-permute-start(bf16[2,256,256]{2,1,0:T(8,128)(2,1)S(1)} %get-tuple-element.7), channel_id=1, source_target_pairs={{0,1},{1,0},{2,3},{3,2},{4,5},{5,4},{6,7},{7,6},{8,15},{9,10},{10,... | collective-permute-start | bytes 786440 | tf_op jit(solution)/shard_map/ppermute | solution.py:175
  16.0 8.3 %collective-permute-start.1 = (bf16[2,256,256]{2,1,0:T(8,128)(2,1)S(1)}, bf16[2,256,256]{2,1,0:T(8,128)(2,1)S(1)}, u32[]{:S(2)}, u32[]{:S(2)}) collective-permute-start(bf16[2,256,256]{2,1,0:T(8,128)(2,1)S(1)} %get-tuple-element.9), channel_id=1, source_target_pairs={{0,1},{1,0},{2,3},{3,2},{4,5},{5,4},{6,7},{7,6},{8,15},{9,10},{10,... | collective-permute-start | bytes 786440 | tf_op jit(solution)/shard_map/ppermute | solution.py:174
  19.8 10.9 %collective-permute-start.4 = (bf16[256,256]{1,0:T(8,128)(2,1)S(1)}, bf16[256,256]{1,0:T(8,128)(2,1)S(1)}, u32[]{:S(2)}, u32[]{:S(2)}) collective-permute-start(bf16[256,256]{1,0:T(8,128)(2,1)S(1)} %fusion.6), channel_id=1, source_target_pairs={{0,6},{1,7},{2,0},{3,1},{4,2},{5,3},{6,4},{7,5},{8,14},{9,15},{10,... | collective-permute-start | bytes 393224 | tf_op jit(solution)/shard_map/ppermute | solution.py:179
  24.4 11.7 %collective-permute-start.3 = (bf16[256,256]{1,0:T(8,128)(2,1)S(1)}, bf16[256,256]{1,0:T(8,128)(2,1)S(1)}, u32[]{:S(2)}, u32[]{:S(2)}) collective-permute-start(bf16[256,256]{1,0:T(8,128)(2,1)S(1)} %get-tuple-element.12), channel_id=1, source_target_pairs={{0,2},{1,3},{2,4},{3,5},{4,6},{5,7},{6,0},{7,1},{8,10},{9,11},{10,... | collective-permute-start | bytes 393224 | tf_op jit(solution)/shard_map/ppermute | solution.py:179
  26.4 13.2 %collective-permute-start.2 = (bf16[256,256]{1,0:T(8,128)(2,1)S(1)}, bf16[256,256]{1,0:T(8,128)(2,1)S(1)}, u32[]{:S(2)}, u32[]{:S(2)}) collective-permute-start(bf16[256,256]{1,0:T(8,128)(2,1)S(1)} %get-tuple-element.13), channel_id=1, source_target_pairs={{0,4},{1,5},{2,6},{3,7},{4,0},{5,1},{6,2},{7,3},{8,12},{9,13},{10,... | collective-permute-start | bytes 393224 | tf_op jit(solution)/shard_map/ppermute | solution.py:179
  40.6 23.1 %all-to-all-start = ((bf16[64,8,256]{2,1,0:T(8,128)(2,1)}), bf16[64,8,256]{2,1,0:T(8,128)(2,1)S(1)}, u32[]{:S(2)}, u32[]{:S(2)}) async-start(bf16[64,8,256]{2,1,0:T(8,128)(2,1)} %bitcast.38), calls=%async_computation | async-start | bytes 524288 | tf_op jit(solution)/shard_map/all_to_all | solution.py:198

commit v3 on v2

--- a/solution.py
+++ b/solution.py
@@ -19,7 +19,7 @@
         odd = lax.rem(ten + lax.axis_index("replica"), 2)
         ten = lax.rem(ten + jnp.where(odd == 0, 1, n_ten - 1), n_ten)
     side = lax.rem(ten, 2)
-    return [lax.rem(ten // 2 + apart, count) * 2 + side for apart in (2, 1, count - 1, 0)]
+    return [lax.rem(ten // 2 + apart, count) * 2 + side for apart in (1, count - 1, 2, 0)]
 
 
 def project_body(features_ref, weight_ref, *refs):
@@ -179,9 +179,9 @@
         return lax.ppermute(outward, "tensor", [(z, (z + 2 * step) % n_ten) for z in range(n_ten)])
 
     arrivals = (
-        onward(kept_a[0], got_a[0], 2),
-        onward(kept_a[1], got_a[1], 1),
-        onward(kept_b[0], got_b[0], quarter - 1),
+        onward(kept_a[0], got_a[0], 1),
+        onward(kept_a[1], got_a[1], quarter - 1),
+        onward(kept_b[0], got_b[0], 2),
     )
 
     owners = image_owner.reshape(n_rep, images)

time: 65 us -> 62.4 us (0.960)
  waiting for transfers between devices: 20.8 us -> 18.5 us
    ppermute x3, waiting for transfers between devices: 8.87 us -> 7.43 us  [onward(): lax.ppermute(outward, 'tensor', [(z, (z + 2 * step) % n_ten) for z in ran...]
    all_to_all x1, starting transfers between devices: 11.1 us -> 9.91 us  [local(): lax.all_to_all(outgoing, 'replica', split_axis=0, concat_axis=0, tiled=True)]
    ppermute x1, waiting for transfers between devices: 0.89 us -> 0.01 us  [local(): got_a = lax.ppermute(sent_a, both, neighbours)]
    ppermute x3, starting transfers between devices: 9.85 us -> 10.7 us  [onward(): lax.ppermute(outward, 'tensor', [(z, (z + 2 * step) % n_ten) for z in ran...]
  transfers between devices with their start and end apart: 6 -> 6, of which waited for: 5 -> 4; matrix products, arithmetic and copies ran while one was open for 4% -> 4% of each run, Pallas kernels for 0% -> 0%
where the time goes in v3:
time: 62.4 us; the launch traced here: 62 us
  starting transfers between devices  34 us (54%)
  waiting for transfers between devices  18.5 us (30%)
  Pallas kernels  5.88 us (9%)
  matrix products  1.25 us (2%)
  between operations  0.87 us (1%)
  other arithmetic  0.85 us (1%)
  local copies, waits for them, and re-layouts  0.67 us (1%)
    ppermute x1, starting transfers between devices, local(): got_b = lax.ppermute(sent_b, both, neighbours)  11.5 us
    all_to_all x1, waiting for transfers between devices, local(): lax.all_to_all(outgoing, 'replica', split_axis=0, concat_axis=0, tiled=True)  10.8 us
    ppermute x3, starting transfers between devices, onward(): lax.ppermute(outward, 'tensor', [(z, (z + 2 * step) % n_ten) for z in ran...  10.7 us
    all_to_all x1, starting transfers between devices, local(): lax.all_to_all(outgoing, 'replica', split_axis=0, concat_axis=0, tiled=True)  9.91 us
    ppermute x3, waiting for transfers between devices, onward(): lax.ppermute(outward, 'tensor', [(z, (z + 2 * step) % n_ten) for z in ran...  7.43 us
    pallas_call x1, Pallas kernels, project(): pl.pallas_call(project_body, in_specs=[pl.BlockSpec(memory_space=pltpu.HB...  3.84 us
    ppermute x1, starting transfers between devices, local(): got_a = lax.ppermute(sent_a, both, neighbours)  1.92 us
  transfers between devices with their start and end apart: 6, of which 4 were waited for; matrix products, arithmetic and copies ran while one was open for 4% of the time, Pallas kernels for 0%

profile of v3, /device:TPU:1, one launch (start us, length us, event | category | flops | bytes accessed | tf_op | source)
XLA Modules:
  0.0 62.0 jit_solution(3989375642750991166)
XLA Ops:
  0.7 3.8 %shard_map.104 = (bf16[2,256,256]{2,1,0:T(8,128)(2,1)S(1)}, bf16[2,256,256]{2,1,0:T(8,128)(2,1)S(1)}, bf16[2,256,256]{2,1,0:T(8,128)(2,1)S(1)}, bf16[2,256,256]{2,1,0:T(8,128)(2,1)S(1)}) custom-call(bf16[64,4,960]{2,1,0:T(4,128)(2,1)} %features_ref.1, bf16[960,8,256]{2,1,0:T(8,128)(2,1)} %weight_ref.1), custom_call_target="tpu_custom_call" | custom-call | tf_op jit(solution)/shard_map/pallas_call | solution.py:65
  4.6 11.5 %collective-permute-start = (bf16[2,256,256]{2,1,0:T(8,128)(2,1)S(1)}, bf16[2,256,256]{2,1,0:T(8,128)(2,1)S(1)}, u32[]{:S(2)}, u32[]{:S(2)}) collective-permute-start(bf16[2,256,256]{2,1,0:T(8,128)(2,1)S(1)} %get-tuple-element.7), channel_id=1, source_target_pairs={{0,1},{1,0},{2,3},{3,2},{4,5},{5,4},{6,7},{7,6},{8,15},{9,10},{10,... | collective-permute-start | bytes 786440 | tf_op jit(solution)/shard_map/ppermute | solution.py:175
  16.0 1.9 %collective-permute-start.1 = (bf16[2,256,256]{2,1,0:T(8,128)(2,1)S(1)}, bf16[2,256,256]{2,1,0:T(8,128)(2,1)S(1)}, u32[]{:S(2)}, u32[]{:S(2)}) collective-permute-start(bf16[2,256,256]{2,1,0:T(8,128)(2,1)S(1)} %get-tuple-element.9), channel_id=1, source_target_pairs={{0,1},{1,0},{2,3},{3,2},{4,5},{5,4},{6,7},{7,6},{8,15},{9,10},{10,... | collective-permute-start | bytes 786440 | tf_op jit(solution)/shard_map/ppermute | solution.py:174
  18.0 0.1 iota_compare_fusion.2
  18.2 0.2 convert_reduce_fusion
  18.4 0.2 reduce_window_sum.11
  18.8 0.3 fusion.15
  19.1 0.1 fusion.10
  19.2 0.1 select_reduce_fusion
  19.4 0.1 add.59.slot_ref
  19.5 0.3 collective-permute-done
  19.8 4.5 %collective-permute-start.4 = (bf16[256,256]{1,0:T(8,128)(2,1)S(1)}, bf16[256,256]{1,0:T(8,128)(2,1)S(1)}, u32[]{:S(2)}, u32[]{:S(2)}) collective-permute-start(bf16[256,256]{1,0:T(8,128)(2,1)S(1)} %fusion.6), channel_id=1, source_target_pairs={{0,4},{1,5},{2,6},{3,7},{4,0},{5,1},{6,2},{7,3},{8,12},{9,13},{10,... | collective-permute-start | bytes 393224 | tf_op jit(solution)/shard_map/ppermute | solution.py:179
  24.5 1.9 %collective-permute-start.3 = (bf16[256,256]{1,0:T(8,128)(2,1)S(1)}, bf16[256,256]{1,0:T(8,128)(2,1)S(1)}, u32[]{:S(2)}, u32[]{:S(2)}) collective-permute-start(bf16[256,256]{1,0:T(8,128)(2,1)S(1)} %get-tuple-element.12), channel_id=1, source_target_pairs={{0,6},{1,7},{2,0},{3,1},{4,2},{5,3},{6,4},{7,5},{8,14},{9,15},{10,... | collective-permute-start | bytes 393224 | tf_op jit(solution)/shard_map/ppermute | solution.py:179
  26.4 4.3 %collective-permute-start.2 = (bf16[256,256]{1,0:T(8,128)(2,1)S(1)}, bf16[256,256]{1,0:T(8,128)(2,1)S(1)}, u32[]{:S(2)}, u32[]{:S(2)}) collective-permute-start(bf16[256,256]{1,0:T(8,128)(2,1)S(1)} %get-tuple-element.13), channel_id=1, source_target_pairs={{0,2},{1,3},{2,4},{3,5},{4,6},{5,7},{6,0},{7,1},{8,10},{9,11},{10,... | collective-permute-start | bytes 393224 | tf_op jit(solution)/shard_map/ppermute | solution.py:179
  30.7 2.8 %collective-permute-done.4.c_ref = bf16[256,256]{1,0:T(8,128)(2,1)S(1)} collective-permute-done((bf16[256,256]{1,0:T(8,128)(2,1)S(1)}, bf16[256,256]{1,0:T(8,128)(2,1)S(1)}, u32[]{:S(2)}, u32[]{:S(2)}) %collective-permute-start.4) | collective-permute-done | bytes 131104 | tf_op jit(solution)/shard_map/ppermute | solution.py:179
  33.5 4.6 %collective-permute-done.3.b_ref = bf16[256,256]{1,0:T(8,128)(2,1)S(1)} collective-permute-done((bf16[256,256]{1,0:T(8,128)(2,1)S(1)}, bf16[256,256]{1,0:T(8,128)(2,1)S(1)}, u32[]{:S(2)}, u32[]{:S(2)}) %collective-permute-start.3) | collective-permute-done | bytes 131104 | tf_op jit(solution)/shard_map/ppermute | solution.py:179
  38.1 1.0 %shard_map.105 = bf16[512,256]{1,0:T(8,128)(2,1)} custom-call(s32[1,256]{1,0:T(1,128)S(1)} %add.59.slot_ref, bf16[256,256]{1,0:T(8,128)(2,1)S(1)} %slice_bitcast_fusion.5.kept_ref, bf16[256,256]{1,0:T(8,128)(2,1)S(1)} %slice_bitcast_fusion.4.got_ref, bf16[256,256]{1,0:T(8,128)(2,1)S(1)} %collective-permute-done.2.a_ref, ...), custom_call_target="tpu_custom_call" | custom-call | tf_op jit(solution)/shard_map/pallas_call | solution.py:100
  39.1 9.9 %all-to-all-start = ((bf16[64,8,256]{2,1,0:T(8,128)(2,1)}), bf16[64,8,256]{2,1,0:T(8,128)(2,1)S(1)}, u32[]{:S(2)}, u32[]{:S(2)}) async-start(bf16[64,8,256]{2,1,0:T(8,128)(2,1)} %bitcast.38), calls=%async_computation | async-start | bytes 524288 | tf_op jit(solution)/shard_map/all_to_all | solution.py:198
  49.0 0.1 copy.15
  49.1 0.1 broadcast_in_dim.18
  49.3 0.1 reshape_reshape.4.tag_ref
  49.4 0.8 %fusion.3 = bf16[8,8,128]{2,1,0:T(8,128)(2,1)} fusion(bf16[8,128,1,256]{3,1,0,2:T(8,128)(2,1)S(1)} %bitcast.41, f32[8,8]{1,0:T(8,128)S(1)} %get-tuple-element.15, f32[8,128]{1,0:T(8,128)S(1)} %get-tuple-element.16, f32[8,8]{1,0:T(8,128)S(1)} %get-tuple-element.14, bf16[8,8,128]{2,1,0:T(8,128)(2,1)S(1)} %get-tuple-element.19), kind=kOutput, calls=%fused_computation.5 | convolution fusion | flops 2129920 | bytes 307200 | tf_op jit(solution)/shard_map/bkgs,bskd->bkgd/dot_general | solution.py:222
  50.2 10.8 %all-to-all-done = bf16[64,8,256]{2,1,0:T(8,128)(2,1)S(1)} async-done(((bf16[64,8,256]{2,1,0:T(8,128)(2,1)}), bf16[64,8,256]{2,1,0:T(8,128)(2,1)S(1)}, u32[]{:S(2)}, u32[]{:S(2)}) %all-to-all-start) | async-done | bytes 262176 | tf_op jit(solution)/shard_map/all_to_all | solution.py:198
  61.0 1.0 %shard_map.106 = bf16[8,8,128]{2,1,0:T(8,128)(2,1)} custom-call(s32[1,512]{1,0:T(1,128)S(1)} %reshape_reshape.4.tag_ref, bf16[8,8,128]{2,1,0:T(8,128)(2,1)S(1)} %copy-done.1, bf16[512,256]{1,0:T(8,128)(2,1)S(1)} %bitcast.37), custom_call_target="tpu_custom_call" | custom-call | tf_op jit(solution)/shard_map/pallas_call | solution.py:134
  (30 shorter events, 0.4 us)
Async XLA Ops:
  0.6 18.1 %copy-start = (bf16[8,8,128]{2,1,0:T(8,128)(2,1)S(1)}, bf16[8,8,128]{2,1,0:T(8,128)(2,1)}, u32[]{:S(2)}) copy-start(bf16[8,8,128]{2,1,0:T(8,128)(2,1)} %param.14) | copy-start | bytes 49156
  0.6 17.3 %copy-start.6 = (s32[8]{0:T(128)S(1)}, s32[8]{0:T(128)}, u32[]{:S(2)}) copy-start(s32[8]{0:T(128)} %param.17) | copy-start | bytes 100
  0.7 17.4 %copy-start.4 = (bf16[8,1,256]{2,0,1:T(8,128)(2,1)S(1)}, bf16[8,1,256]{2,0,1:T(8,128)(2,1)}, u32[]{:S(2)}) copy-start(bf16[8,1,256]{2,0,1:T(8,128)(2,1)} %param.16) | copy-start | bytes 12292
  0.7 17.4 %copy-start.2 = (s32[4096]{0:T(1024)S(1)}, s32[4096]{0:T(1024)}, u32[]{:S(2)}) copy-start(s32[4096]{0:T(1024)} %param.11) | copy-start | bytes 49156
  0.7 18.0 %copy-start.3 = (s32[4096]{0:T(1024)S(1)}, s32[4096]{0:T(1024)}, u32[]{:S(2)}) copy-start(s32[4096]{0:T(1024)} %param.12) | copy-start | bytes 49156
  0.7 18.1 %copy-start.5 = (bf16[8,128,1,256]{3,1,2,0:T(8,128)(2,1)S(1)}, bf16[8,128,1,256]{3,1,2,0:T(8,128)(2,1)}, u32[]{:S(2)}) copy-start(bf16[8,128,1,256]{3,1,2,0:T(8,128)(2,1)} %param.15) | copy-start | bytes 1572868
  0.7 60.3 %copy-start.1 = (bf16[8,8,128]{2,1,0:T(8,128)(2,1)S(1)}, bf16[8,8,128]{2,1,0:T(8,128)(2,1)}, u32[]{:S(2)}) copy-start(bf16[8,8,128]{2,1,0:T(8,128)(2,1)} %query_ref.1) | copy-start | bytes 49156
  4.6 15.2 %collective-permute-start = (bf16[2,256,256]{2,1,0:T(8,128)(2,1)S(1)}, bf16[2,256,256]{2,1,0:T(8,128)(2,1)S(1)}, u32[]{:S(2)}, u32[]{:S(2)}) collective-permute-start(bf16[2,256,256]{2,1,0:T(8,128)(2,1)S(1)} %get-tuple-element.7), channel_id=1, source_target_pairs={{0,1},{1,0},{2,3},{3,2},{4,5},{5,4},{6,7},{7,6},{8,15},{9,10},{10,... | collective-permute-start | bytes 786440 | tf_op jit(solution)/shard_map/ppermute | solution.py:175
  16.0 8.3 %collective-permute-start.1 = (bf16[2,256,256]{2,1,0:T(8,128)(2,1)S(1)}, bf16[2,256,256]{2,1,0:T(8,128)(2,1)S(1)}, u32[]{:S(2)}, u32[]{:S(2)}) collective-permute-start(bf16[2,256,256]{2,1,0:T(8,128)(2,1)S(1)} %get-tuple-element.9), channel_id=1, source_target_pairs={{0,1},{1,0},{2,3},{3,2},{4,5},{5,4},{6,7},{7,6},{8,15},{9,10},{10,... | collective-permute-start | bytes 786440 | tf_op jit(solution)/shard_map/ppermute | solution.py:174
  19.8 13.6 %collective-permute-start.4 = (bf16[256,256]{1,0:T(8,128)(2,1)S(1)}, bf16[256,256]{1,0:T(8,128)(2,1)S(1)}, u32[]{:S(2)}, u32[]{:S(2)}) collective-permute-start(bf16[256,256]{1,0:T(8,128)(2,1)S(1)} %fusion.6), channel_id=1, source_target_pairs={{0,4},{1,5},{2,6},{3,7},{4,0},{5,1},{6,2},{7,3},{8,12},{9,13},{10,... | collective-permute-start | bytes 393224 | tf_op jit(solution)/shard_map/ppermute | solution.py:179
  24.5 13.6 %collective-permute-start.3 = (bf16[256,256]{1,0:T(8,128)(2,1)S(1)}, bf16[256,256]{1,0:T(8,128)(2,1)S(1)}, u32[]{:S(2)}, u32[]{:S(2)}) collective-permute-start(bf16[256,256]{1,0:T(8,128)(2,1)S(1)} %get-tuple-element.12), channel_id=1, source_target_pairs={{0,6},{1,7},{2,0},{3,1},{4,2},{5,3},{6,4},{7,5},{8,14},{9,15},{10,... | collective-permute-start | bytes 393224 | tf_op jit(solution)/shard_map/ppermute | solution.py:179
  26.4 11.7 %collective-permute-start.2 = (bf16[256,256]{1,0:T(8,128)(2,1)S(1)}, bf16[256,256]{1,0:T(8,128)(2,1)S(1)}, u32[]{:S(2)}, u32[]{:S(2)}) collective-permute-start(bf16[256,256]{1,0:T(8,128)(2,1)S(1)} %get-tuple-element.13), channel_id=1, source_target_pairs={{0,2},{1,3},{2,4},{3,5},{4,6},{5,7},{6,0},{7,1},{8,10},{9,11},{10,... | collective-permute-start | bytes 393224 | tf_op jit(solution)/shard_map/ppermute | solution.py:179
  39.1 21.9 %all-to-all-start = ((bf16[64,8,256]{2,1,0:T(8,128)(2,1)}), bf16[64,8,256]{2,1,0:T(8,128)(2,1)S(1)}, u32[]{:S(2)}, u32[]{:S(2)}) async-start(bf16[64,8,256]{2,1,0:T(8,128)(2,1)} %bitcast.38), calls=%async_computation | async-start | bytes 524288 | tf_op jit(solution)/shard_map/all_to_all | solution.py:198
